TPU v7x, 32 devices: a whole 2x2x4 slice. The times are simulated.
32 devices in a mesh: row: 4 (over z), col: 8 (over y, x, core).
Axes of the slice: x: 2, y: 2, z: 4, core: 2. Of those that a mesh axis runs over, the one named last changes fastest.
Arguments:
- spectra: bfloat16 [1024, 32, 128], P(('row', 'col')), may hold values from -6 to 6
- pair_bins: int32 [1024, 1024], P('row', 'col'), may hold values from 0 to 255
- row_subs: int32 [4, 16], P('row'), may hold values from 0 to 31, as said below
- station_subs: int32 [1024, 8], replicated, may hold values from 0 to 31, as said below
- kernel: bfloat16 [32, 256, 256], replicated, may hold values from -0.375 to 0.375
Outputs:
- spectrum: float32 [32, 32, 256], P(('row', 'col'))
Inputs may be any that keep to these rules, and one draw needn't show every extreme that they name: `row_subs`: each row lists 16 distinct subarrays; each subarray is listed for exactly two row blocks. `station_subs`: each station names 8 distinct subarrays, all listed in row_subs for the station's row block.
All inputs are finite; a program needn't handle non-finite values.
Results may differ from a plain program's by a relative error of at most 0.0039.
Values may be sent and summed in bfloat16 or wider, within the bound.
A program may use at most 64 MiB of HBM per device.

v0:
```python
import math
import jax
import jax.numpy as jnp
from jax import lax
from jax.sharding import PartitionSpec as P

F = 32
NBIN = 256
SUB_DEV = 1


def spread_rows(slot_terms, slot_subs, row_count):
    targets = jnp.arange(row_count, dtype=jnp.int32)
    selector = (targets[:, None] == slot_subs[None, :]).astype(jnp.float32)
    return jnp.dot(selector, slot_terms, precision=lax.Precision.HIGHEST)


def project(owned_bins, kernel):
    velocity_power = jnp.einsum(
        "sfb,fbv->sfv", owned_bins, kernel, preferred_element_type=jnp.float32
    )
    scale = lax.rsqrt(jnp.mean(velocity_power * velocity_power, axis=2, keepdims=True) + 1e-06)
    return velocity_power * scale


def on_device(spectra, pair_bins, row_subs, station_subs, kernel):
    shard_rows = spectra.shape[0]
    col_total = lax.axis_size("col")
    row_index = lax.axis_index("row")
    col_index = lax.axis_index("col")
    row_spectra = lax.all_gather(spectra, "col", axis=0, tiled=True)
    col_spectra = lax.all_gather(spectra, "row", axis=0, tiled=True)
    row_span = row_spectra.shape[0]
    col_span = col_spectra.shape[0]
    slot_subs = row_subs[0]
    slot_count = slot_subs.shape[0]
    row_members = lax.dynamic_slice_in_dim(station_subs, row_index * row_span, row_span, 0)
    positions = jnp.arange(col_span, dtype=jnp.int32)
    col_ids = (
        positions // shard_rows * col_total + col_index
    ) * shard_rows + positions % shard_rows
    col_members = jnp.take(station_subs, col_ids, axis=0)
    row_mask = jnp.any(row_members[None, :, :] == slot_subs[:, None, None], axis=2).astype(
        jnp.bfloat16
    )
    col_mask = jnp.any(col_members[None, :, :] == slot_subs[:, None, None], axis=2).astype(
        jnp.bfloat16
    )
    cross_spec = jnp.einsum(
        "aft,jft->faj", row_spectra, col_spectra, preferred_element_type=jnp.float32
    ).astype(jnp.bfloat16)
    step_rows = math.gcd(row_span, max(1, 2048 // col_span))
    step_count = row_span // step_rows
    bin_ids = jnp.arange(NBIN, dtype=jnp.int32)

    def accumulate(step_index, running):
        first_row = step_index * step_rows
        cross_part = lax.dynamic_slice_in_dim(cross_spec, first_row, step_rows, 1)
        mask_part = lax.dynamic_slice_in_dim(row_mask, first_row, step_rows, 1)
        bins_part = lax.dynamic_slice_in_dim(pair_bins, first_row, step_rows, 0)
        weighted = mask_part[:, None, :, None] * col_mask[:, None, None, :] * cross_part[None]
        onehot = (bins_part.reshape(-1, 1) == bin_ids[None, :]).astype(jnp.bfloat16)
        return running + jnp.dot(
            weighted.reshape(slot_count * F, step_rows * col_span),
            onehot,
            preferred_element_type=jnp.float32,
        )

    partial_value = lax.fori_loop(
        0, step_count, accumulate, jnp.zeros((slot_count * F, NBIN), jnp.float32)
    )
    partial_value = partial_value.reshape(slot_count, F, NBIN)
    freq_part = lax.psum_scatter(partial_value, "col", scatter_dimension=1, tiled=True)
    freq_share = freq_part.shape[1]
    group_rows = SUB_DEV * col_total
    summed = lax.psum_scatter(
        spread_rows(
            freq_part.reshape(slot_count, freq_share * NBIN),
            slot_subs,
            lax.axis_size("row") * group_rows,
        ),
        "row",
        scatter_dimension=0,
        tiled=True,
    )
    binned = summed.reshape(group_rows, freq_share, NBIN).astype(jnp.bfloat16)
    return project(lax.all_to_all(binned, "col", split_axis=0, concat_axis=1, tiled=True), kernel)


def solution(mesh):
    in_specs = (P(("row", "col"), None, None), P("row", "col"), P("row", None), P(), P())
    out_specs = P(("row", "col"), None, None)
    return jax.shard_map(
        on_device, mesh=mesh, in_specs=in_specs, out_specs=out_specs, check_vma=False
    )
```

profile of v0, /device:TPU:0, one launch (start us, length us, event | category | flops | bytes accessed | tf_op | source)
XLA Modules:
  0.0 180.9 jit_solution(14719300169441912463)
XLA Ops:
  6.5 1.8 copy.29
  9.2 1.0 copy.27
  10.1 0.7 constant_dynamic-slice_fusion.2
  10.8 0.8 compare_reduce_fusion
  12.6 27.1 %all-gather.5.cloned.1.call-done = bf16[128,32,128]{2,0,1:T(8,128)(2,1)} async-done(((bf16[32,32,128]{2,0,1:T(8,128)(2,1)}), bf16[128,32,128]{2,0,1:T(8,128)(2,1)}) %all-gather.5.cloned.1.call-update) | async-done | bytes 1048592 | tf_op jit(solution)/shard_map/all_gather | solution.py:32
  39.6 29.4 %all-gather.3.cloned.1.call-done = bf16[256,32,128]{2,0,1:T(8,128)(2,1)} async-done(((bf16[32,32,128]{2,0,1:T(8,128)(2,1)}), bf16[256,32,128]{2,0,1:T(8,128)(2,1)}) %all-gather.3.cloned.1.call-update) | async-done | bytes 2097168 | tf_op jit(solution)/shard_map/all_gather | solution.py:31
  69.0 2.6 %convolution_convert_fusion = bf16[32,256,128]{2,1,0:T(8,128)(2,1)S(1)} fusion(bf16[256,32,128]{2,0,1:T(8,128)(2,1)} %all-gather.3.cloned.1.call-done, bf16[128,32,128]{2,0,1:T(8,128)(2,1)} %all-gather.5.cloned.1.call-done), kind=kOutput, calls=%fused_computation.13 | convolution fusion | flops 269484032 | bytes 5242880 | tf_op jit(solution)/shard_map/aft,jft->faj/dot_general | solution.py:49
  71.6 33.1 %while.14 = (s32[]{:T(128)}, f32[512,256]{1,0:T(8,128)S(1)}, bf16[16,256]{1,0:T(8,128)(2,1)S(1)}, bf16[16,128]{1,0:T(8,128)(2,1)S(1)}, bf16[32,256,128]{2,1,0:T(...) while((s32[]{:T(128)}, f32[512,256]{1,0:T(8,128)S(1)}, ...), condition=%wide.region_3.4_spmd.clone, body=%wide.region_2.3_spmd.clone.sunk | while | flops 538738688 | bytes 5797553 | solution.py:69
  72.7 1.0 fusion.31
  74.8 1.0 fusion.31
  76.8 1.0 fusion.31
  78.9 1.0 fusion.31
  81.0 1.0 fusion.31
  83.0 1.0 fusion.31
  85.1 1.0 fusion.31
  87.2 1.0 fusion.31
  89.3 1.0 fusion.31
  91.3 1.0 fusion.31
  93.4 1.0 fusion.31
  95.5 1.0 fusion.31
  97.5 1.0 fusion.31
  99.6 1.0 fusion.31
  101.7 1.0 fusion.31
  103.8 1.0 fusion.31
  104.8 1.1 copy.31
  105.9 34.2 %reduce-scatter.3.cloned.1.call-done = f32[16,4,256]{2,0,1:T(8,128)} async-done(((f32[16,32,256]{2,0,1:T(8,128)}), f32[16,4,256]{2,0,1:T(8,128)}) %reduce-scatter.3.cloned.1.call-update) | async-done | bytes 65552 | tf_op jit(solution)/shard_map/reduce_scatter | solution.py:73
  140.2 0.8 copy.37
  141.0 0.8 fusion.11
  141.9 19.9 %reduce-scatter.5.cloned.1.call-done = f32[8,1024]{1,0:T(8,128)} async-done(((f32[32,1024]{1,0:T(8,128)}), f32[8,1024]{1,0:T(8,128)}) %reduce-scatter.5.cloned.1.call-update) | async-done | bytes 32784 | tf_op jit(solution)/shard_map/reduce_scatter | solution.py:76
  161.7 0.8 convert_element_type.22
  162.5 8.2 %all_to_all.4 = bf16[8,4,256]{2,1,0:T(4,128)(2,1)S(1)} all-to-all(bf16[8,4,256]{2,1,0:T(4,128)(2,1)S(1)} %copy.33), channel_id=1, replica_groups=mesh['row'=4,'col'=8] {'col'}, dimensions={0} | all-to-all | bytes 32768 | tf_op jit(solution)/shard_map/all_to_all | solution.py:87
  170.7 2.8 %fusion.22 = f32[32,1,256]{2,1,0:T(1,128)S(1)} fusion(bf16[32,256,1]{1,2,0:T(2,128)(2,1)S(1)} %reshape.159, bf16[32,256,256]{2,1,0:T(8,128)(2,1)} %param.11), kind=kOutput, calls=%fused_computation.49 | convolution fusion | flops 4194304 | bytes 4243456 | tf_op jit(solution)/shard_map/sfb,fbv->sfv/dot_general | solution.py:19
  (105 shorter events, 19.3 us)
Async XLA Ops:
  6.5 5.9 %copy-start = (s32[1,16]{1,0:T(1,128)S(1)}, s32[1,16]{1,0:T(1,128)}, u32[]{:S(2)}) copy-start(s32[1,16]{1,0:T(1,128)} %param.9) | copy-start | bytes 196
  6.5 33.1 %all-gather.5.cloned.1.call-start = ((), (), s32[]{:S(2)}) async-start(), calls=%async_computation.4 | async-start | bytes 1310720 | tf_op jit(solution)/shard_map/all_gather | solution.py:32
  8.3 60.7 %all-gather.3.cloned.1.call-start = ((), (), s32[]{:S(2)}) async-start(), calls=%async_computation.3 | async-start | bytes 2359296 | tf_op jit(solution)/shard_map/all_gather | solution.py:31
  9.1 131.1 %reduce-scatter.3.cloned.1.call-start = ((), (), s32[]{:S(2)}) async-start(), calls=%async_computation.5 | async-start | bytes 589824 | tf_op jit(solution)/shard_map/reduce_scatter | solution.py:73
  105.9 55.8 %reduce-scatter.5.cloned.1.call-start = ((), (), s32[]{:S(2)}) async-start(), calls=%async_computation.6 | async-start | bytes 163840 | tf_op jit(solution)/shard_map/reduce_scatter | solution.py:76
Sparse Core Ops, SparseCore 0:
  8.9 30.6 all-gather.4
  41.5 27.4 all-gather.2
  106.0 34.1 reduce-scatter.2
  142.3 19.4 reduce-scatter.4
where the time goes:
time: 182 us; the launch traced here: 181 us
  waiting for transfers between devices  111 us (61%)
  matrix products  21.9 us (12%)
  local copies, waits for them, and re-layouts  19 us (10%)
  between operations  13.2 us (7%)
  blocking collectives  8.21 us (5%)
  other arithmetic  6.36 us (3%)
    reduce_scatter x1, waiting for transfers between devices, on_device(): lax.psum_scatter(partial_value, 'col', scatter_dimension=1, tiled=True)  34.2 us
    all_gather x1, waiting for transfers between devices, on_device(): row_spectra = lax.all_gather(spectra, 'col', axis=0, tiled=True)  29.4 us
    all_gather x1, waiting for transfers between devices, on_device(): col_spectra = lax.all_gather(spectra, 'row', axis=0, tiled=True)  27.1 us
    reduce_scatter x1, waiting for transfers between devices, on_device(): lax.psum_scatter(spread_rows(freq_part.reshape(slot_count, freq_share * N...  19.9 us
    dot_general x16, matrix products, accumulate(): jnp.dot(weighted.reshape(slot_count * F, step_rows * col_span), onehot, p...  15.6 us
    eq x16, local copies, waits for them, and re-layouts, accumulate(): onehot = (bins_part.reshape(-1, 1) == bin_ids[None, :]).astype(jnp.bfloat16)  11.2 us
    all_to_all x1, blocking collectives, on_device(): lax.all_to_all(binned, 'col', split_axis=0, concat_axis=1, tiled=True)  8.21 us
    mul x32, other arithmetic, accumulate(): mask_part[:, None, :, None] * col_mask[:, None, None, :] * cross_part[None]  3.76 us
  transfers between devices with their start and end apart: 4, of which 4 were waited for; matrix products, arithmetic and copies ran while one was open for 2% of the time, Pallas kernels for 0%

commit v1 on v0

--- a/solution.py
+++ b/solution.py
@@ -7,6 +7,18 @@
 F = 32
 NBIN = 256
 SUB_DEV = 1
+
+
+def collect(x, axis, dim):
+    ways, here, hop = (lax.axis_size(axis), lax.axis_index(axis), x.shape[dim])
+    line, have = (x, 1)
+    while have < ways:
+        line = jnp.concatenate(
+            [line, lax.ppermute(line, axis, [(d, (d - have) % ways) for d in range(ways)])],
+            axis=dim,
+        )
+        have = 2 * have
+    return jnp.roll(line, here * hop, axis=dim)
 
 
 def spread_rows(slot_terms, slot_subs, row_count):
@@ -29,7 +41,7 @@
     row_index = lax.axis_index("row")
     col_index = lax.axis_index("col")
     row_spectra = lax.all_gather(spectra, "col", axis=0, tiled=True)
-    col_spectra = lax.all_gather(spectra, "row", axis=0, tiled=True)
+    col_spectra = collect(spectra, "row", 0)
     row_span = row_spectra.shape[0]
     col_span = col_spectra.shape[0]
     slot_subs = row_subs[0]

time: 182 us -> 179 us (0.984)
  waiting for transfers between devices: 111 us -> 80.4 us
  local copies, waits for them, and re-layouts: 19 us -> 38 us
  starting transfers between devices: 0.12 us -> 6.58 us
  other arithmetic: 6.36 us -> 8.23 us
    all_gather x1, waiting for transfers between devices: 29.4 us -> 0.01 us  [on_device(): row_spectra = lax.all_gather(spectra, 'col', axis=0, tiled=True)]
    all_gather x1 -> x0, waiting for transfers between devices: 27.1 us -> none  [on_device(): col_spectra = lax.all_gather(spectra, 'row', axis=0, tiled=True)]
    ppermute x0 -> x2, waiting for transfers between devices: none -> 26.2 us  [collect(): lax.ppermute(line, axis, [(d, (d - have) % ways) for d in range(ways)])]
    dynamic_slice x16, local copies, waits for them, and re-layouts: 0.43 us -> 14.9 us  [accumulate(): cross_part = lax.dynamic_slice_in_dim(cross_spec, first_row, step_rows, 1)]
    ppermute x0 -> x2, starting transfers between devices: none -> 6.49 us  [collect(): lax.ppermute(line, axis, [(d, (d - have) % ways) for d in range(ways)])]
    unnamed x4 -> x15, local copies, waits for them, and re-layouts: 2.74 us -> 7.2 us
  transfers between devices with their start and end apart: 4 -> 5, of which waited for: 4 -> 4; matrix products, arithmetic and copies ran while one was open for 2% -> 3% of each run, Pallas kernels for 0% -> 0%
where the time goes in v1:
time: 179 us; the launch traced here: 177 us
  waiting for transfers between devices  80.4 us (45%)
  local copies, waits for them, and re-layouts  38 us (21%)
  matrix products  21.9 us (12%)
  between operations  13.3 us (7%)
  other arithmetic  8.23 us (5%)
  blocking collectives  8.2 us (5%)
  starting transfers between devices  6.58 us (4%)
    reduce_scatter x1, waiting for transfers between devices, on_device(): lax.psum_scatter(partial_value, 'col', scatter_dimension=1, tiled=True)  34.1 us
    ppermute x2, waiting for transfers between devices, collect(): lax.ppermute(line, axis, [(d, (d - have) % ways) for d in range(ways)])  26.2 us
    reduce_scatter x1, waiting for transfers between devices, on_device(): lax.psum_scatter(spread_rows(freq_part.reshape(slot_count, freq_share * N...  20 us
    dot_general x16, matrix products, accumulate(): jnp.dot(weighted.reshape(slot_count * F, step_rows * col_span), onehot, p...  15.6 us
    dynamic_slice x16, local copies, waits for them, and re-layouts, accumulate(): cross_part = lax.dynamic_slice_in_dim(cross_spec, first_row, step_rows, 1)  14.9 us
    eq x16, local copies, waits for them, and re-layouts, accumulate(): onehot = (bins_part.reshape(-1, 1) == bin_ids[None, :]).astype(jnp.bfloat16)  11.3 us
    all_to_all x1, blocking collectives, on_device(): lax.all_to_all(binned, 'col', split_axis=0, concat_axis=1, tiled=True)  8.2 us
    unnamed x15, local copies, waits for them, and re-layouts  7.2 us
  transfers between devices with their start and end apart: 5, of which 4 were waited for; matrix products, arithmetic and copies ran while one was open for 3% of the time, Pallas kernels for 0%

profile of v1, /device:TPU:0, one launch (start us, length us, event | category | flops | bytes accessed | tf_op | source)
XLA Modules:
  0.0 177.3 jit_solution(8464911716811761680)
XLA Ops:
  6.5 1.8 %constant_dynamic-update-slice_fusion.5 = (bf16[256,32,128]{2,0,1:T(8,128)(2,1)S(1)}, bf16[32,32,128]{2,0,1:T(8,128)(2,1)}) fusion(bf16[32,32,128]{2,1,0:T(8,128)(2,1)} %param.7), kind=kLoop, calls=%fused_computation.30 | loop fusion | bytes 786432
  8.4 5.1 %collective-permute-start = (bf16[32,32,128]{2,0,1:T(8,128)(2,1)}, bf16[32,32,128]{2,0,1:T(8,128)(2,1)S(1)}, u32[]{:S(2)}, u32[]{:S(2)}) collective-permute-start(bf16[32,32,128]{2,0,1:T(8,128)(2,1)} %get-tuple-element.196), channel_id=1, source_target_pairs={{0,24},{8,0},{16,8},{24,16},{1,25},{9,1},{17,9},{25,17},{2,26},{10... | collective-permute-start | bytes 786440 | tf_op jit(solution)/shard_map/ppermute | solution.py:17
  15.0 1.0 copy.43
  16.7 2.7 %collective-permute-done = bf16[32,32,128]{2,0,1:T(8,128)(2,1)S(1)} collective-permute-done((bf16[32,32,128]{2,0,1:T(8,128)(2,1)}, bf16[32,32,128]{2,0,1:T(8,128)(2,1)S(1)}, u32[]{:S(2)}, u32[]{:S(2)}) %collective-permute-start) | collective-permute-done | bytes 262176 | tf_op jit(solution)/shard_map/ppermute | solution.py:17
  19.4 1.8 %pad_maximum_fusion = bf16[64,32,128]{2,0,1:T(8,128)(2,1)} fusion(bf16[32,32,128]{2,0,1:T(8,128)(2,1)S(1)} %collective-permute-done, bf16[32,32,128]{2,0,1:T(8,128)(2,1)} %get-tuple-element.196), kind=kLoop, calls=%fused_computation.15 | loop fusion | flops 1048576 | bytes 1048576 | tf_op jit(solution)/shard_map/concatenate | solution.py:16
  21.2 1.4 collective-permute-start.1
  23.0 23.4 %collective-permute-done.1 = bf16[64,32,128]{2,0,1:T(8,128)(2,1)S(1)} collective-permute-done((bf16[64,32,128]{2,0,1:T(8,128)(2,1)}, bf16[64,32,128]{2,0,1:T(8,128)(2,1)S(1)}, u32[]{:S(2)}, u32[]{:S(2)}) %collective-permute-start.1) | collective-permute-done | bytes 524320 | tf_op jit(solution)/shard_map/ppermute | solution.py:17
  46.7 1.3 copy-done.1
  48.0 2.6 %convert_bitcast_fusion = bf16[32,256,128]{1,2,0:T(8,128)(2,1)S(1)} fusion(bf16[256,32,128]{2,0,1:T(8,128)(2,1)} %all-gather.2.cloned.1.call-done, bf16[256,32,128]{2,0,1:T(8,128)(2,1)} %copy-done.1, s32[]{:T(128)S(6)} %select_n.90), kind=kOutput, calls=%fused_computation.13 | convolution fusion | flops 269484032 | bytes 5242884 | tf_op jit(solution)/shard_map/aft,jft->faj/dot_general | solution.py:61
  50.7 2.9 %copy.50 = bf16[32,256,128]{2,1,0:T(8,128)(2,1)} copy(bf16[32,256,128]{1,2,0:T(8,128)(2,1)S(1)} %convert_bitcast_fusion) | data formatting | bytes 4194304
  53.6 47.6 %while.14 = (s32[]{:T(128)}, f32[512,256]{1,0:T(8,128)S(1)}, bf16[16,256]{1,0:T(8,128)(2,1)S(1)}, bf16[16,128]{1,0:T(8,128)(2,1)S(1)}, bf16[32,256,128]{2,1,0:T(...) while((s32[]{:T(128)}, f32[512,256]{1,0:T(8,128)S(1)}, ...), condition=%wide.region_3.4_spmd.clone, body=%wide.region_2.3_spmd.clone.sunk | while | flops 538738688 | bytes 5797545 | solution.py:81
  55.5 1.0 fusion.32
  58.5 1.0 fusion.32
  61.5 1.0 fusion.32
  64.5 1.0 fusion.32
  67.4 1.0 fusion.32
  70.4 1.0 fusion.32
  73.4 1.0 fusion.32
  76.4 1.0 fusion.32
  79.3 1.0 fusion.32
  82.3 1.0 fusion.32
  85.3 1.0 fusion.32
  88.3 1.0 fusion.32
  91.2 1.0 fusion.32
  94.2 1.0 fusion.32
  97.2 1.0 fusion.32
  100.1 1.0 fusion.32
  101.1 1.1 copy.51
  102.3 34.1 %reduce-scatter.3.cloned.1.call-done = f32[16,4,256]{2,0,1:T(8,128)} async-done(((f32[16,32,256]{2,0,1:T(8,128)}), f32[16,4,256]{2,0,1:T(8,128)}) %reduce-scatter.3.cloned.1.call-update) | async-done | bytes 65552 | tf_op jit(solution)/shard_map/reduce_scatter | solution.py:85
  138.1 20.0 %reduce-scatter.5.cloned.1.call-done = f32[8,1024]{1,0:T(8,128)} async-done(((f32[32,1024]{1,0:T(8,128)}), f32[8,1024]{1,0:T(8,128)}) %reduce-scatter.5.cloned.1.call-update) | async-done | bytes 32784 | tf_op jit(solution)/shard_map/reduce_scatter | solution.py:88
  158.9 8.2 %all_to_all.4 = bf16[8,4,256]{2,1,0:T(4,128)(2,1)S(1)} all-to-all(bf16[8,4,256]{2,1,0:T(4,128)(2,1)S(1)} %copy.53), channel_id=1, replica_groups=mesh['row'=4,'col'=8] {'col'}, dimensions={0} | all-to-all | bytes 32768 | tf_op jit(solution)/shard_map/all_to_all | solution.py:99
  167.1 2.8 %fusion.24 = f32[32,1,256]{2,1,0:T(1,128)S(1)} fusion(bf16[32,256,1]{1,2,0:T(2,128)(2,1)S(1)} %reshape.159, bf16[32,256,256]{2,1,0:T(8,128)(2,1)} %param.11), kind=kOutput, calls=%fused_computation.58 | convolution fusion | flops 4194304 | bytes 4243456 | tf_op jit(solution)/shard_map/sfb,fbv->sfv/dot_general | solution.py:31
  (119 shorter events, 37.4 us)
Async XLA Ops:
  6.5 16.2 %copy-start.3 = (s32[1,16]{1,0:T(1,128)S(1)}, s32[1,16]{1,0:T(1,128)}, u32[]{:S(2)}) copy-start(s32[1,16]{1,0:T(1,128)} %param.9) | copy-start | bytes 196
  6.5 41.5 %all-gather.2.cloned.1.call-start = ((), (), s32[]{:S(2)}) async-start(), calls=%async_computation.3 | async-start | bytes 2359296 | tf_op jit(solution)/shard_map/all_gather | solution.py:43
  8.4 38.1 %copy-start = (bf16[32,32,128]{2,1,0:T(8,128)(2,1)S(1)}, bf16[32,32,128]{2,1,0:T(8,128)(2,1)}, u32[]{:S(2)}) copy-start(bf16[32,32,128]{2,1,0:T(8,128)(2,1)} %param.7) | copy-start | bytes 786436
  8.4 128.1 %reduce-scatter.3.cloned.1.call-start = ((), (), s32[]{:S(2)}) async-start(), calls=%async_computation.4 | async-start | bytes 589824 | tf_op jit(solution)/shard_map/reduce_scatter | solution.py:85
  8.4 11.0 %collective-permute-start = (bf16[32,32,128]{2,0,1:T(8,128)(2,1)}, bf16[32,32,128]{2,0,1:T(8,128)(2,1)S(1)}, u32[]{:S(2)}, u32[]{:S(2)}) collective-permute-start(bf16[32,32,128]{2,0,1:T(8,128)(2,1)} %get-tuple-element.196), channel_id=1, source_target_pairs={{0,24},{8,0},{16,8},{24,16},{1,25},{9,1},{17,9},{25,17},{2,26},{10... | collective-permute-start | bytes 786440 | tf_op jit(solution)/shard_map/ppermute | solution.py:17
  21.2 25.2 %collective-permute-start.1 = (bf16[64,32,128]{2,0,1:T(8,128)(2,1)}, bf16[64,32,128]{2,0,1:T(8,128)(2,1)S(1)}, u32[]{:S(2)}, u32[]{:S(2)}) collective-permute-start(bf16[64,32,128]{2,0,1:T(8,128)(2,1)} %pad_maximum_fusion), channel_id=1, source_target_pairs={{0,16},{8,24},{16,0},{24,8},{1,17},{9,25},{17,1},{25,9},{2,18},{10... | collective-permute-start | bytes 1572872 | tf_op jit(solution)/shard_map/ppermute | solution.py:17
  46.7 1.3 copy-start.1
  50.7 2.9 %copy-start.2 = (f32[512,256]{1,0:T(8,128)S(1)}, f32[512,256]{1,0:T(8,128)}, u32[]{:S(2)}) copy-start(f32[512,256]{1,0:T(8,128)} %custom-call) | copy-start | bytes 1572868
  102.3 55.9 %reduce-scatter.5.cloned.1.call-start = ((), (), s32[]{:S(2)}) async-start(), calls=%async_computation.5 | async-start | bytes 163840 | tf_op jit(solution)/shard_map/reduce_scatter | solution.py:88
Sparse Core Ops, SparseCore 0:
  9.2 30.8 all-gather.1
  102.4 34.0 reduce-scatter.2
  138.7 19.4 reduce-scatter.4
